TPU v7x, 256 devices: a whole 4x4x8 slice. The times are simulated.
256 devices in a mesh: ctx: 64 (over z, x, core), head: 4 (over y).
Axes of the slice: x: 4, y: 4, z: 8, core: 2. Of those that a mesh axis runs over, the one named last changes fastest.
Arguments:
- inputs: bfloat16 [12288, 2048], P('ctx'), may hold values from -6 to 6
- projection: bfloat16 [3, 2048, 1024], P(None, None, 'head'), may hold values from -0.125 to 0.125
- conv_weight: float32 [3, 4, 1024], P(None, None, 'head'), may hold values from -3 to 3
- gate_code: int32 [8, 12288], P('head', 'ctx'), may hold values from 0 to 1023
- beta_code: int32 [8, 12288], P('head', 'ctx'), may hold values from 0 to 1023
- grad_out: bfloat16 [12288, 1024], P('ctx', 'head'), may hold values from -6 to 6
Outputs:
- input_grad: bfloat16 [12288, 2048], P(('ctx', 'head'))
- kernel_grad: float32 [3, 4, 1024], P(None, None, 'head')
All inputs are finite; a program needn't handle non-finite values.
Results may differ from a plain program's by a relative error of at most 0.0068.
The roundings to bfloat16 on the way count: a program that leaves them out, or rounds other values in their place, can miss the bound.
Values may be sent and summed in bfloat16 or wider, within the bound.
No kernel may reach another device: no remote copies, remote signals or barrier semaphores. Data moves between devices by JAX's collectives and lax.ppermute only.
A program may use at most 64 MiB of HBM per device.

v0:
```python
import jax
import jax.numpy as jnp
from jax import lax
from jax.sharding import PartitionSpec as P

DK = 128
KW = 4
GROUP = 64
HIGHEST_PRECISION = lax.Precision.HIGHEST


def from_behind(block, axis, distance):
    devices = range(lax.axis_size(axis))
    route = [(i - distance, i) for i in devices if i - distance in devices]
    return lax.ppermute(block, axis, route)


def normalize(matrix):
    return matrix * lax.rsqrt(jnp.sum(matrix * matrix, -1, keepdims=True) + 1e-06)


def features(extended, weights):
    length = extended.shape[1] - (KW - 1)
    convolved = weights[:, 0:1, :] * extended[:, 0:length, :]
    for offset in range(1, KW):
        convolved = (
            convolved
            + weights[:, offset : offset + 1, :] * extended[:, offset : offset + length, :]
        )
    activated = jax.nn.silu(convolved)
    head_count = activated.shape[2] // DK
    activated = activated.reshape(3, length, head_count, DK).transpose(0, 2, 1, 3)
    queries = normalize(activated[0]) * DK ** (-0.5)
    norm_keys = normalize(activated[1])
    return (queries, norm_keys, activated[2])


def block_step(carried, pieces):
    queries, norm_keys, value_rows, log_gate, beta_rate = pieces
    cumulative = jnp.cumsum(log_gate, axis=-1)
    decay_now = jnp.exp(cumulative)
    between = cumulative[:, :, None] - cumulative[:, None, :]
    position = jnp.arange(log_gate.shape[-1])
    strict = position[:, None] > position[None, :]
    inclusive = position[:, None] >= position[None, :]
    key_gram = jnp.einsum("htd,hsd->hts", norm_keys, norm_keys, precision=HIGHEST_PRECISION)
    lower_part = jnp.where(strict, jnp.exp(between), 0.0) * key_gram * beta_rate[:, :, None]
    recalled = jnp.einsum("htd,hvd->htv", norm_keys, carried, precision=HIGHEST_PRECISION)
    target = beta_rate[:, :, None] * (value_rows - decay_now[:, :, None] * recalled)
    pseudo = jax.scipy.linalg.solve_triangular(lower_part, target, lower=True, unit_diagonal=True)
    scores = jnp.einsum(
        "htd,hsd->hts", queries, norm_keys, precision=HIGHEST_PRECISION
    ) * jnp.where(inclusive, jnp.exp(between), 0.0)
    outputs = decay_now[:, :, None] * jnp.einsum(
        "htd,hvd->htv", queries, carried, precision=HIGHEST_PRECISION
    )
    outputs = outputs + jnp.einsum("hts,hsv->htv", scores, pseudo, precision=HIGHEST_PRECISION)
    group_total = cumulative[:, -1]
    remaining = jnp.exp(group_total[:, None] - cumulative)
    new_state = jnp.exp(group_total)[:, None, None] * carried
    new_state = new_state + jnp.einsum(
        "hsv,hsd->hvd", pseudo, remaining[:, :, None] * norm_keys, precision=HIGHEST_PRECISION
    )
    return (new_state, outputs)


def run_blocks(queries, norm_keys, value_rows, log_gate, beta_rate, carried):
    head_count = queries.shape[0]
    length = queries.shape[1]
    blocks = length // GROUP

    def to_blocks(tensor):
        return jnp.moveaxis(
            tensor.reshape((tensor.shape[0], blocks, GROUP) + tensor.shape[2:]), 1, 0
        )

    final_state, outputs = lax.scan(
        block_step,
        carried,
        (
            to_blocks(queries),
            to_blocks(norm_keys),
            to_blocks(value_rows),
            to_blocks(log_gate),
            to_blocks(beta_rate),
        ),
    )
    outputs = jnp.moveaxis(outputs, 0, 1).reshape(head_count, length, DK)
    return (outputs, final_state)


def chain_product(left_side, right_side):
    return jnp.einsum("hij,hjk->hik", left_side, right_side, precision=HIGHEST_PRECISION)


def on_device(inputs, projection, conv_weight, gate_code, beta_code, grad_out):
    length = inputs.shape[0]
    head_count = gate_code.shape[0]
    projected = jnp.stack(
        [
            jnp.dot(inputs, projection[member], preferred_element_type=jnp.float32)
            for member in range(3)
        ]
    ).astype(jnp.bfloat16)
    tail_rows = projected[:, length - (KW - 1) :, :]
    earlier_rows = from_behind(tail_rows, "ctx", 1)
    extended = jnp.concatenate([earlier_rows, projected], 1).astype(jnp.float32)
    log_gate = jnp.log(1.0 - 0.001 * gate_code.astype(jnp.float32) / 1023.0)
    beta_rate = beta_code.astype(jnp.float32) / 1023.0
    (queries, norm_keys, value_rows), feature_pull = jax.vjp(features, extended, conv_weight)
    identity = jnp.broadcast_to(jnp.eye(DK, dtype=jnp.float32), (head_count, DK, DK))
    zero_state = jnp.zeros((head_count, DK, DK), jnp.float32)
    paired = run_blocks(
        jnp.concatenate([queries, queries], 0),
        jnp.concatenate([norm_keys, norm_keys], 0),
        jnp.concatenate([value_rows, jnp.zeros_like(value_rows)], 0),
        jnp.concatenate([log_gate, log_gate], 0),
        jnp.concatenate([beta_rate, beta_rate], 0),
        jnp.concatenate([zero_state, identity], 0),
    )[1]
    local_state = paired[:head_count]
    transition = paired[head_count:]

    def advance(rounds, carried):
        return from_behind(chain_product(carried, transition) + local_state, "ctx", 1)

    entering = lax.fori_loop(0, lax.axis_size("ctx") - 1, advance, zero_state)

    def core(query_part, key_part, value_part, start_state):
        return run_blocks(query_part, key_part, value_part, log_gate, beta_rate, start_state)

    (outputs, leaving), core_pull = jax.vjp(core, queries, norm_keys, value_rows, entering)
    cotangent = grad_out.astype(jnp.float32).reshape(length, head_count, DK).transpose(1, 0, 2)
    direct_grads = core_pull((cotangent, zero_state))
    local_adjoint = direct_grads[3]
    flipped = jnp.swapaxes(transition, 1, 2)

    def retreat(rounds, carried):
        return from_behind(chain_product(carried, flipped) + local_adjoint, "ctx", -1)

    arriving = lax.fori_loop(0, lax.axis_size("ctx") - 1, retreat, zero_state)
    carried_grads = core_pull((jnp.zeros_like(outputs), arriving))
    feature_grads = tuple((direct_grads[member] + carried_grads[member] for member in range(3)))
    extended_grad, weight_grad = feature_pull(feature_grads)
    spill_rows = extended_grad[:, : KW - 1, :]
    returned = from_behind(spill_rows, "ctx", -1)
    raw_grad = extended_grad[:, KW - 1 :, :]
    raw_grad = raw_grad.at[:, length - (KW - 1) :, :].add(returned)
    rounded = raw_grad.astype(jnp.bfloat16)
    input_grad = lax.psum_scatter(
        jnp.einsum("mtc,mdc->td", rounded, projection, preferred_element_type=jnp.float32),
        "head",
        scatter_dimension=0,
        tiled=True,
    ).astype(jnp.bfloat16)
    kernel_grad = lax.psum(weight_grad, "ctx")
    return (input_grad, kernel_grad)


def solution(mesh):
    return jax.shard_map(
        on_device,
        mesh=mesh,
        in_specs=(
            P("ctx", None),
            P(None, None, "head"),
            P(None, None, "head"),
            P("head", "ctx"),
            P("head", "ctx"),
            P("ctx", "head"),
        ),
        out_specs=(P(("ctx", "head"), None), P(None, None, "head")),
        check_vma=False,
    )
```

profile of v0, /device:TPU:136, one launch (start us, length us, event | category | flops | bytes accessed | tf_op | source)
XLA Modules:
  0.0 1999.5 jit_solution(9301813911177826447)
XLA Ops:
  27.6 80.2 %while.114 = (s32[]{:T(128)}, f32[4,128,128]{2,1,0:T(8,128)S(1)}, f32[3,4,64]{2,0,1:T(4,128)S(1)}, f32[3,4,64,128]{3,2,0,1:T(8,128)}, f32[3,4,64]{2,0,1:T(4,128)...) while((s32[]{:T(128)}, f32[4,128,128]{2,1,0:T(8,128)S(1)}, f32[3,4,64]{2,0,1:T(4,128)S(1)}, ...), condition=%wide.region_3.4_spmd, body=%wide.region_1.0_spmd.sunk | while | flops 151388224 | bytes 2060989 | solution.py:77
  32.0 20.4 %custom-call.38 = f32[4,1,64,64]{2,3,1,0:T(8,128)S(1)} custom-call(f32[4,1,64,64]{3,2,1,0:T(8,128)} %fusion.344), custom_call_target="InvertDiagBlocksLowerTriangular" | custom-call | tf_op jit(solution)/shard_map/while/body/eval_jaxpr/jit(_solve_triangular)/vmap()/triangular_solve | solution.py:50
  58.7 20.4 %custom-call.38 = f32[4,1,64,64]{2,3,1,0:T(8,128)S(1)} custom-call(f32[4,1,64,64]{3,2,1,0:T(8,128)} %fusion.344), custom_call_target="InvertDiagBlocksLowerTriangular" | custom-call | tf_op jit(solution)/shard_map/while/body/eval_jaxpr/jit(_solve_triangular)/vmap()/triangular_solve | solution.py:50
  85.4 20.4 %custom-call.38 = f32[4,1,64,64]{2,3,1,0:T(8,128)S(1)} custom-call(f32[4,1,64,64]{3,2,1,0:T(8,128)} %fusion.344), custom_call_target="InvertDiagBlocksLowerTriangular" | custom-call | tf_op jit(solution)/shard_map/while/body/eval_jaxpr/jit(_solve_triangular)/vmap()/triangular_solve | solution.py:50
  114.6 737.0 %while.115 = (s32[]{:T(128)}, f32[2,128,128]{2,1,0:T(8,128)S(1)}, f32[2,128,128]{2,1,0:T(8,128)}, f32[2,128,128]{2,1,0:T(8,128)}, s32[]{:T(128)}) while((s32[]{:T(128)}, f32[2,128,128]{2,1,0:T(8,128)S(1)}, f32[2,128,128]{2,1,0:T(8,128)}, f32[2,128,128]{2,1,0:T(8,128)}, s32[]{:T(128)}) %tuple.256), condition=%wide.region_5.6_spmd, body=%wide.region_4.5_spmd.sunk | while | flops 50364416 | bytes 1048677 | solution.py:127
  176.9 7.9 collective-permute-done
  188.6 7.9 collective-permute-done
  212.0 7.9 collective-permute-done
  282.2 7.9 collective-permute-done
  305.6 7.9 collective-permute-done
  851.7 66.0 %while.118 = (s32[]{:T(128)}, f32[2,128,128]{2,1,0:T(8,128)S(1)}, f32[3,2,64,64]{3,2,1,0:T(8,128)}, f32[3,2,64,1]{2,1,3,0:T(2,128)S(1)}, f32[3,2,128,128]{3,2,1,...) while((s32[]{:T(128)}, f32[2,128,128]{2,1,0:T(8,128)S(1)}, ...), condition=%wide.region_9.10_spmd.clone.clone, body=%wide.region_7.9_spmd.clone.clone.sunk | while | flops 88346816 | bytes 2166041 | solution.py:77
  856.4 11.2 custom-call.40
  878.3 11.2 custom-call.40
  900.3 11.2 custom-call.40
  919.8 62.7 %while.119 = (s32[]{:T(128)}, f32[2,128,128]{2,1,0:T(8,128)S(1)}, f32[3,2,64,128]{3,2,0,1:T(8,128)}, f32[3,2,64,128]{3,2,0,1:T(8,128)}, f32[3,2,64,128]{3,2,0,1:...) while((s32[]{:T(128)}, f32[2,128,128]{2,1,0:T(8,128)S(1)}, ...), condition=%wide.region_11.13_spmd.clone, body=%wide.region_10.12_spmd.clone.sunk | while | flops 258445376 | bytes 4060456 | solution.py:77
  923.0 9.8 custom-call.41
  943.9 9.8 custom-call.41
  964.8 9.8 custom-call.41
  982.5 674.3 %while.116 = (s32[]{:T(128)}, f32[2,128,128]{2,1,0:T(8,128)S(1)}, f32[2,128,128]{2,1,0:T(8,128)}, f32[2,128,128]{2,1,0:T(8,128)S(1)}, s32[]{:T(128)}) while((s32[]{:T(128)}, f32[2,128,128]{2,1,0:T(8,128)S(1)}, f32[2,128,128]{2,1,0:T(8,128)}, f32[2,128,128]{2,1,0:T(8,128)S(1)}, s32[]{:T(128)}) %tuple.265), condition=%wide.region_13.15_spmd, body=%wide.region_12.14_spmd.sunk | while | flops 50364416 | bytes 1048677 | solution.py:141
  1658.9 62.7 %while.117 = (s32[]{:T(128)}, f32[2,128,128]{2,1,0:T(8,128)S(1)}, f32[3,2,64,128]{3,2,0,1:T(8,128)}, f32[3,2,64,128]{3,2,0,1:T(8,128)}, f32[3,2,64,128]{3,2,0,1:...) while((s32[]{:T(128)}, f32[2,128,128]{2,1,0:T(8,128)S(1)}, ...), condition=%wide.region_15.17_spmd.clone, body=%wide.region_14.16_spmd.clone.sunk | while | flops 258314432 | bytes 3794713 | solution.py:77
  1662.1 9.8 custom-call.39
  1683.1 9.8 custom-call.39
  1704.0 9.8 custom-call.39
  1739.2 251.2 %psum.7 = f32[3,4,256]{2,0,1:T(4,128)S(1)} all-reduce(f32[3,4,256]{2,0,1:T(4,128)S(1)} %pad_add_fusion.1), channel_id=1, replica_groups=mesh['ctx'=64,'head'=4] {'ctx'}, use_global_device_ids=true, to_apply=%region_23.25 | all-reduce | flops 3072 | bytes 24576 | tf_op jit(solution)/shard_map/psum | solution.py:156
  (734 shorter events, 1537.2 us)
Async XLA Ops:
  7.2 1983.8 %reduce-scatter.2.cloned.1.call-start = ((), (), s32[]{:S(2)}) async-start(), calls=%async_computation.1 | async-start | bytes 1966080 | tf_op jit(solution)/shard_map/reduce_scatter | solution.py:150
  116.5 9.8 collective-permute-start
  128.2 9.8 collective-permute-start
  139.9 9.8 collective-permute-start
  163.3 9.8 collective-permute-start
  175.0 9.8 collective-permute-start
  186.7 9.8 collective-permute-start
  198.4 9.8 collective-permute-start
  210.1 9.8 collective-permute-start
  221.8 9.8 collective-permute-start
  233.5 9.8 collective-permute-start
  256.9 9.8 collective-permute-start
  280.3 9.8 collective-permute-start
  292.0 9.8 collective-permute-start
  303.7 9.8 collective-permute-start
  315.4 9.8 collective-permute-start
  327.1 9.8 collective-permute-start
  350.5 9.8 collective-permute-start
  385.6 9.8 collective-permute-start
  397.3 9.8 collective-permute-start
  409.0 9.8 collective-permute-start
  420.7 9.8 collective-permute-start
  432.4 9.8 collective-permute-start
  444.1 9.8 collective-permute-start
  (129 other events, 3523.0 us)
Sparse Core Ops, SparseCore 0:
  1739.3 28.3 reduce-scatter.1
where the time goes:
time: 2010 us; the launch traced here: 2000 us
  waiting for transfers between devices  659 us (33%)
  starting transfers between devices  571 us (28%)
  matrix products  287 us (14%)
  blocking collectives  251 us (12%)
  other arithmetic  181 us (9%)
  local copies, waits for them, and re-layouts  32.3 us (2%)
    ppermute x128, waiting for transfers between devices, from_behind(): return lax.ppermute(block, axis, route)  659 us
    ppermute x128, starting transfers between devices, from_behind(): return lax.ppermute(block, axis, route)  571 us
    psum x1, blocking collectives, on_device(): kernel_grad = lax.psum(weight_grad, 'ctx')  251 us
    dot_general x126, matrix products, chain_product(): jnp.einsum('hij,hjk->hik', left_side, right_side, precision=HIGHEST_PRECI...  193 us
    another operation x45, other arithmetic, block_step(): jax.scipy.linalg.solve_triangular(lower_part, target, lower=True, unit_di...  162 us
  transfers between devices with their start and end apart: 129, of which 128 were waited for; matrix products, arithmetic and copies ran while one was open for 0% of the time, Pallas kernels for 0%

commit v1 on v0

--- a/solution.py
+++ b/solution.py
@@ -153,7 +153,7 @@
         scatter_dimension=0,
         tiled=True,
     ).astype(jnp.bfloat16)
-    kernel_grad = lax.psum(weight_grad, "ctx")
+    kernel_grad = jnp.sum(lax.all_gather(weight_grad, "ctx"), axis=0)
     return (input_grad, kernel_grad)
 
 

time: 2010 us -> 1810 us (0.900)
  blocking collectives: 251 us -> 50.1 us
    psum x1 -> x0, blocking collectives: 251 us -> none  [on_device(): kernel_grad = lax.psum(weight_grad, 'ctx')]
    all_gather x0 -> x1, blocking collectives: none -> 50.1 us  [on_device(): kernel_grad = jnp.sum(lax.all_gather(weight_grad, 'ctx'), axis=0)]
where the time goes in v1:
time: 1810 us; the launch traced here: 1800 us
  waiting for transfers between devices  659 us (36%)
  starting transfers between devices  571 us (32%)
  matrix products  287 us (16%)
  other arithmetic  181 us (10%)
  blocking collectives  50.1 us (3%)
  local copies, waits for them, and re-layouts  31.7 us (2%)
    ppermute x128, waiting for transfers between devices, from_behind(): return lax.ppermute(block, axis, route)  659 us
    ppermute x128, starting transfers between devices, from_behind(): return lax.ppermute(block, axis, route)  571 us
    dot_general x126, matrix products, chain_product(): jnp.einsum('hij,hjk->hik', left_side, right_side, precision=HIGHEST_PRECI...  193 us
    another operation x45, other arithmetic, block_step(): jax.scipy.linalg.solve_triangular(lower_part, target, lower=True, unit_di...  162 us
    all_gather x1, blocking collectives, on_device(): kernel_grad = jnp.sum(lax.all_gather(weight_grad, 'ctx'), axis=0)  50.1 us
  transfers between devices with their start and end apart: 129, of which 128 were waited for; matrix products, arithmetic and copies ran while one was open for 0% of the time, Pallas kernels for 0%

profile of v1, /device:TPU:136, one launch (start us, length us, event | category | flops | bytes accessed | tf_op | source)
XLA Modules:
  0.0 1798.7 jit_solution(17508646686910683585)
XLA Ops:
  27.6 80.2 %while.114 = (s32[]{:T(128)}, f32[4,128,128]{2,1,0:T(8,128)S(1)}, f32[3,4,64]{2,0,1:T(4,128)S(1)}, f32[3,4,64,128]{3,2,0,1:T(8,128)}, f32[3,4,64]{2,0,1:T(4,128)...) while((s32[]{:T(128)}, f32[4,128,128]{2,1,0:T(8,128)S(1)}, f32[3,4,64]{2,0,1:T(4,128)S(1)}, ...), condition=%wide.region_3.4_spmd, body=%wide.region_1.0_spmd.sunk | while | flops 151388224 | bytes 2060989 | solution.py:77
  32.0 20.4 %custom-call.38 = f32[4,1,64,64]{2,3,1,0:T(8,128)S(1)} custom-call(f32[4,1,64,64]{3,2,1,0:T(8,128)} %fusion.344), custom_call_target="InvertDiagBlocksLowerTriangular" | custom-call | tf_op jit(solution)/shard_map/while/body/eval_jaxpr/jit(_solve_triangular)/vmap()/triangular_solve | solution.py:50
  58.7 20.4 %custom-call.38 = f32[4,1,64,64]{2,3,1,0:T(8,128)S(1)} custom-call(f32[4,1,64,64]{3,2,1,0:T(8,128)} %fusion.344), custom_call_target="InvertDiagBlocksLowerTriangular" | custom-call | tf_op jit(solution)/shard_map/while/body/eval_jaxpr/jit(_solve_triangular)/vmap()/triangular_solve | solution.py:50
  85.4 20.4 %custom-call.38 = f32[4,1,64,64]{2,3,1,0:T(8,128)S(1)} custom-call(f32[4,1,64,64]{3,2,1,0:T(8,128)} %fusion.344), custom_call_target="InvertDiagBlocksLowerTriangular" | custom-call | tf_op jit(solution)/shard_map/while/body/eval_jaxpr/jit(_solve_triangular)/vmap()/triangular_solve | solution.py:50
  114.6 737.0 %while.115 = (s32[]{:T(128)}, f32[2,128,128]{2,1,0:T(8,128)S(1)}, f32[2,128,128]{2,1,0:T(8,128)}, f32[2,128,128]{2,1,0:T(8,128)}, s32[]{:T(128)}) while((s32[]{:T(128)}, f32[2,128,128]{2,1,0:T(8,128)S(1)}, f32[2,128,128]{2,1,0:T(8,128)}, f32[2,128,128]{2,1,0:T(8,128)}, s32[]{:T(128)}) %tuple.259), condition=%wide.region_5.6_spmd, body=%wide.region_4.5_spmd.sunk | while | flops 50364416 | bytes 1048677 | solution.py:127
  212.0 7.9 collective-permute-done
  282.2 7.9 collective-permute-done
  305.6 7.9 collective-permute-done
  399.2 7.9 collective-permute-done
  761.9 7.9 collective-permute-done
  851.7 66.0 %while.118 = (s32[]{:T(128)}, f32[2,128,128]{2,1,0:T(8,128)S(1)}, f32[3,2,64,64]{3,2,1,0:T(8,128)}, f32[3,2,64,1]{2,1,3,0:T(2,128)S(1)}, f32[3,2,128,128]{3,2,1,...) while((s32[]{:T(128)}, f32[2,128,128]{2,1,0:T(8,128)S(1)}, ...), condition=%wide.region_9.10_spmd.clone.clone, body=%wide.region_7.9_spmd.clone.clone.sunk | while | flops 88346816 | bytes 2166041 | solution.py:77
  856.4 11.2 custom-call.40
  878.3 11.2 custom-call.40
  900.3 11.2 custom-call.40
  919.8 62.7 %while.119 = (s32[]{:T(128)}, f32[2,128,128]{2,1,0:T(8,128)S(1)}, f32[3,2,64,128]{3,2,0,1:T(8,128)}, f32[3,2,64,128]{3,2,0,1:T(8,128)}, f32[3,2,64,128]{3,2,0,1:...) while((s32[]{:T(128)}, f32[2,128,128]{2,1,0:T(8,128)S(1)}, ...), condition=%wide.region_11.13_spmd.clone, body=%wide.region_10.12_spmd.clone.sunk | while | flops 258445376 | bytes 4060456 | solution.py:77
  923.0 9.8 custom-call.41
  943.9 9.8 custom-call.41
  964.8 9.8 custom-call.41
  982.5 674.3 %while.116 = (s32[]{:T(128)}, f32[2,128,128]{2,1,0:T(8,128)S(1)}, f32[2,128,128]{2,1,0:T(8,128)}, f32[2,128,128]{2,1,0:T(8,128)S(1)}, s32[]{:T(128)}) while((s32[]{:T(128)}, f32[2,128,128]{2,1,0:T(8,128)S(1)}, f32[2,128,128]{2,1,0:T(8,128)}, f32[2,128,128]{2,1,0:T(8,128)S(1)}, s32[]{:T(128)}) %tuple.268), condition=%wide.region_13.15_spmd, body=%wide.region_12.14_spmd.sunk | while | flops 50364416 | bytes 1048677 | solution.py:141
  1658.9 62.7 %while.117 = (s32[]{:T(128)}, f32[2,128,128]{2,1,0:T(8,128)S(1)}, f32[3,2,64,128]{3,2,0,1:T(8,128)}, f32[3,2,64,128]{3,2,0,1:T(8,128)}, f32[3,2,64,128]{3,2,0,1:...) while((s32[]{:T(128)}, f32[2,128,128]{2,1,0:T(8,128)S(1)}, ...), condition=%wide.region_15.17_spmd.clone, body=%wide.region_14.16_spmd.clone.sunk | while | flops 258314432 | bytes 3794713 | solution.py:77
  1662.1 9.8 custom-call.39
  1683.1 9.8 custom-call.39
  1704.0 9.8 custom-call.39
  1739.3 50.1 %all-gather = f32[192,4,256]{2,1,0:T(4,128)S(1)} all-gather(f32[3,4,256]{2,1,0:T(4,128)S(1)} %pad_add_fusion.2), channel_id=2, replica_groups=mesh['ctx'=64,'head'=4] {'ctx'}, dimensions={0}, use_global_device_ids=true | all-gather | bytes 798720 | tf_op jit(solution)/shard_map/all_gather | solution.py:156
  (738 shorter events, 1537.4 us)
Async XLA Ops:
  7.2 1782.9 %reduce-scatter.2.cloned.1.call-start = ((), (), s32[]{:S(2)}) async-start(), calls=%async_computation.1 | async-start | bytes 1966080 | tf_op jit(solution)/shard_map/reduce_scatter | solution.py:150
  116.5 9.8 collective-permute-start
  128.2 9.8 collective-permute-start
  139.9 9.8 collective-permute-start
  151.6 9.8 collective-permute-start
  175.0 9.8 collective-permute-start
  186.7 9.8 collective-permute-start
  198.4 9.8 collective-permute-start
  210.1 9.8 collective-permute-start
  221.8 9.8 collective-permute-start
  233.5 9.8 collective-permute-start
  256.9 9.8 collective-permute-start
  280.3 9.8 collective-permute-start
  292.0 9.8 collective-permute-start
  303.7 9.8 collective-permute-start
  315.4 9.8 collective-permute-start
  327.1 9.8 collective-permute-start
  350.5 9.8 collective-permute-start
  385.6 9.8 collective-permute-start
  397.3 9.8 collective-permute-start
  409.0 9.8 collective-permute-start
  420.7 9.8 collective-permute-start
  432.4 9.8 collective-permute-start
  444.1 9.8 collective-permute-start
  (129 other events, 3523.0 us)
Sparse Core Ops, SparseCore 0:
  1739.3 28.4 reduce-scatter.1
